TPU v7x, 32 devices: a whole 2x2x4 slice. The times are simulated.
32 devices in a mesh: groups: 2 (over x), track: 4 (over y, core), frame: 4 (over z).
Axes of the slice: x: 2, y: 2, z: 4, core: 2. Of those that a mesh axis runs over, the one named last changes fastest.
Arguments:
- frames: bfloat16 [16, 4096, 256], P(('groups', 'frame')), parts along dimension 0, may hold values from -9 to 9
- query_frame: int32 [1024], P(('groups', 'track')), parts along dimension 0, may hold values from 0 to 7
- query_pixel: int32 [1024], P(('groups', 'track')), parts along dimension 0, may hold values from 0 to 4095
- cotangent: float32 [2, 16, 512], P(None, ('groups', 'frame'), 'track'), parts along dimension 1, may hold values from -48 to 48
Outputs:
- frame_grad: float32 [4096, 16, 256], P('track', ('groups', 'frame')), parts along dimension 1
- query_grad: float32 [1024, 256], P(('groups', 'track', 'frame')), parts along dimension 0
There are 2 independent parts, one for each index of `groups`. A program takes and returns all parts, laid end to end along the dimension named above; each array names one. Nothing has to cross between parts.
All inputs are finite; a program needn't handle non-finite values.
Results may differ from a plain program's by a relative error of at most 0.0029.
Values may be sent and summed in bfloat16 or wider, within the bound.
No kernel may reach another device: no remote copies, remote signals or barrier semaphores. Data moves between devices by JAX's collectives and lax.ppermute only.
A program may use at most 64 MiB of HBM per device.

v0:
```python
import jax
import jax.numpy as jnp
from jax import lax
from jax.sharding import PartitionSpec as P

C = 256
FEAT_H = 64
FEAT_W = 64


def on_device(frames, query_frame, query_pixel, cotangent):
    held_frames = frames.shape[0]
    pixels = frames.shape[1]
    channels = frames.shape[2]
    offset = lax.axis_index("frame") * held_frames
    local_index = query_frame - offset
    inside = (local_index >= 0) & (local_index < held_frames)
    row_index = jnp.clip(local_index, 0, held_frames - 1) * pixels + query_pixel
    picked = frames.reshape(held_frames * pixels, channels)[row_index]
    picked = jnp.where(inside[:, None], picked.astype(jnp.float32), 0.0)
    query_feat = lax.psum(picked.astype(jnp.bfloat16), "frame")
    score_scale = C ** (-0.5)
    pixel_ids = jnp.arange(pixels)
    coord_x = (pixel_ids % FEAT_W * (2.0 / (FEAT_W - 1)) - 1.0).astype(jnp.float32)
    coord_y = (pixel_ids // FEAT_W * (2.0 / (FEAT_H - 1)) - 1.0).astype(jnp.float32)
    scores = (
        jnp.einsum("qc,tpc->tqp", query_feat, frames, preferred_element_type=jnp.float32)
        * score_scale
    )
    peak_score = jnp.max(scores, axis=2, keepdims=True)
    exp_scores = jnp.exp(scores - peak_score)
    weights = exp_scores / jnp.sum(exp_scores, axis=2, keepdims=True)
    expect_x = jnp.sum(weights * coord_x, axis=2)
    expect_y = jnp.sum(weights * coord_y, axis=2)
    grad_x = cotangent[0]
    grad_y = cotangent[1]
    inner_sum = grad_x * expect_x + grad_y * expect_y
    cost_grad = (
        weights
        * (grad_x[:, :, None] * coord_x + grad_y[:, :, None] * coord_y - inner_sum[:, :, None])
        * score_scale
    ).astype(jnp.bfloat16)
    query_term = jnp.einsum("tqp,tpc->qc", cost_grad, frames, preferred_element_type=jnp.float32)
    query_grad = lax.psum_scatter(query_term, "frame", scatter_dimension=0, tiled=True)
    everyone = lax.all_gather(query_feat, "track", axis=0, tiled=True)
    frame_grad = jnp.einsum(
        "tqp,qc->ptc",
        lax.all_to_all(cost_grad, "track", split_axis=2, concat_axis=1, tiled=True),
        everyone,
        preferred_element_type=jnp.float32,
    )
    return (frame_grad, query_grad)


def solution(mesh):
    return jax.shard_map(
        on_device,
        mesh=mesh,
        in_specs=(
            P(("groups", "frame"), None, None),
            P(("groups", "track")),
            P(("groups", "track")),
            P(None, ("groups", "frame"), "track"),
        ),
        out_specs=(P("track", ("groups", "frame"), None), P(("groups", "track", "frame"), None)),
        check_vma=False,
    )
```

profile of v0, /device:TPU:0, one launch (start us, length us, event | category | flops | bytes accessed | tf_op | source)
XLA Modules:
  0.0 114.3 jit_solution(15682147279452416401)
XLA Ops:
  7.2 0.0 all-reduce.2.cloned.1.call-start
  7.2 0.7 compare_and_fusion
  7.9 0.7 compare_select_fusion
  8.6 3.5 %gather_fusion = bf16[128,256]{1,0:T(8,128)(2,1)S(1)} fusion(bf16[8192,256]{1,0:T(8,128)(2,1)} %bitcast.38, s32[1024]{0:T(1024)S(1)} %pad_clamp_fusion), kind=kCustom, calls=%fused_computation | custom fusion | bytes 131584 | tf_op jit(solution)/shard_map/gather | solution.py:19
  12.1 0.7 select_convert_fusion
  12.8 0.0 all-reduce.2.cloned.1.call-update
  12.8 0.7 slice_bitcast_fusion.1
  13.5 36.5 %all-reduce.2.cloned.1.call-done = bf16[128,256]{1,0:T(8,128)(2,1)} async-done(((bf16[128,256]{1,0:T(8,128)(2,1)}), bf16[128,256]{1,0:T(8,128)(2,1)}) %all-reduce.2.cloned.1.call-update) | async-done | bytes 65552 | tf_op jit(solution)/shard_map/psum | solution.py:21
  50.0 0.0 copy-start.1
  50.0 7.0 %multiply_reduce_fusion.1 = (f32[2,128]{1,0:T(2,128)S(1)}, f32[2,128]{1,0:T(2,128)S(1)}, f32[2,128,4096]{2,1,0:T(8,128)}) fusion(f32[4096]{0:T(1024)S(1)} %get-tuple-element.11, f32[4096]{0:T(1024)S(1)} %get-tuple-element.12, bf16[2,4096,256]{2,1,0:T(8,128)(2,1)} %param.4, bf16[128,256]{1,0:T(8,128)(2,1)} %all-reduce.2.cloned.1.call-done), kind=kOutput, calls=%fused_computation.10 | convolution fusion | flops 544219136 | bytes 8488960 | tf_op jit(solution)/shard_map/div | solution.py:32
  57.0 0.0 copy-done.1
  57.0 3.5 %multiply_convert_fusion = bf16[2,128,4096]{2,1,0:T(8,128)(2,1)S(1)} fusion(f32[2,128,4096]{2,1,0:T(8,128)} %get-tuple-element.10, f32[2,128]{1,0:T(2,128)S(1)} %multiply_add_fusion, f32[4096]{0:T(1024)S(1)} %get-tuple-element.12, f32[2,128]{1,0:T(2,128)S(1)} %get-tuple-element.9, f32[4096]{0:T(1024)S(1)} %get-tuple-element.11, f32[2,128]{1,0:T(2,128)S(1)} %get-tuple-element.8), kind=kLoop, calls=%fused_computation.8 | loop fusion | flops 7340032 | bytes 6327296 | tf_op jit(solution)/shard_map/convert_element_type | solution.py:42
  60.5 3.8 %copy.9 = bf16[2,128,4096]{1,0,2:T(2,128)(2,1)} copy(bf16[2,128,4096]{2,1,0:T(8,128)(2,1)S(1)} %multiply_convert_fusion) | data formatting | bytes 4194304 | tf_op jit(solution)/shard_map/convert_element_type | solution.py:42
  64.2 4.4 %all-to-all-start = ((bf16[2,128,4096]{1,0,2:T(2,128)(2,1)}), bf16[2,128,4096]{1,0,2:T(2,128)(2,1)}, u32[]{:S(2)}, u32[]{:S(2)}) async-start(bf16[2,128,4096]{1,0,2:T(2,128)(2,1)} %copy.9), calls=%async_computation | async-start | bytes 4194304 | tf_op jit(solution)/shard_map/all_to_all | solution.py:48
  68.7 0.0 copy-start
  68.7 0.0 reduce-scatter.2.cloned.1.call-start
  68.7 3.6 %convolution_bitcast_fusion.1 = f32[128,256]{1,0:T(8,128)} fusion(bf16[2,128,4096]{2,1,0:T(8,128)(2,1)S(1)} %multiply_convert_fusion, bf16[2,4096,256]{2,1,0:T(8,128)(2,1)} %param.4), kind=kOutput, calls=%fused_computation.12 | convolution fusion | flops 536870912 | bytes 6422528 | tf_op jit(solution)/shard_map/tqp,tpc->qc/dot_general | solution.py:43
  72.3 0.0 reduce-scatter.2.cloned.1.call-update
  72.3 0.0 copy-done
  72.3 24.2 %all_gather.3 = bf16[512,256]{1,0:T(8,128)(2,1)S(1)} all-gather(bf16[128,256]{1,0:T(8,128)(2,1)S(1)} %copy-done), channel_id=1, replica_groups=mesh['groups'=2,'track'=4,'frame'=4] {'track'}, dimensions={0}, use_global_device_ids=true | all-gather | bytes 327680 | tf_op jit(solution)/shard_map/all_gather | solution.py:45
  96.6 0.0 all-to-all-done
  96.6 4.7 %copy.10 = bf16[2,128,4,1024]{3,1,2,0:T(8,128)(2,1)S(1)} copy(bf16[2,128,4,1024]{1,0,3,2:T(2,128)(2,1)} %bitcast.6) | data formatting | bytes 4194304 | tf_op jit(solution)/shard_map/all_to_all | solution.py:48
  101.3 2.1 %convolution_bitcast_fusion = f32[1024,2,256]{0,2,1:T(8,128)} fusion(bf16[2,512,1024]{2,1,0:T(8,128)(2,1)S(1)} %bitcast.37, bf16[512,256]{1,0:T(8,128)(2,1)S(1)} %all_gather.3), kind=kOutput, calls=%fused_computation.11 | convolution fusion | flops 536870912 | bytes 4456448 | tf_op jit(solution)/shard_map/tqp,qc->ptc/dot_general | solution.py:46
  103.4 4.1 %copy.12 = f32[1024,2,256]{2,1,0:T(2,128)} copy(f32[1024,2,256]{0,2,1:T(8,128)} %convolution_bitcast_fusion) | data formatting | bytes 4194304
  (4 shorter events, 0.0 us)
Async XLA Ops:
  7.2 42.8 %all-reduce.2.cloned.1.call-start = ((), (), s32[]{:S(2)}) async-start(), calls=%async_computation.2 | async-start | bytes 131072 | tf_op jit(solution)/shard_map/psum | solution.py:21
  50.0 7.0 %copy-start.1 = (f32[2,2,128]{2,1,0:T(2,128)S(1)}, f32[2,2,128]{2,1,0:T(2,128)}, u32[]{:S(2)}) copy-start(f32[2,2,128]{2,1,0:T(2,128)} %param.7) | copy-start | bytes 6148
  64.2 32.3 %all-to-all-start = ((bf16[2,128,4096]{1,0,2:T(2,128)(2,1)}), bf16[2,128,4096]{1,0,2:T(2,128)(2,1)}, u32[]{:S(2)}, u32[]{:S(2)}) async-start(bf16[2,128,4096]{1,0,2:T(2,128)(2,1)} %copy.9), calls=%async_computation | async-start | bytes 4194304 | tf_op jit(solution)/shard_map/all_to_all | solution.py:48
  68.7 3.6 %copy-start = (bf16[128,256]{1,0:T(8,128)(2,1)S(1)}, bf16[128,256]{1,0:T(8,128)(2,1)}, u32[]{:S(2)}) copy-start(bf16[128,256]{1,0:T(8,128)(2,1)} %all-reduce.2.cloned.1.call-done) | copy-start | bytes 196612
  68.7 38.8 %reduce-scatter.2.cloned.1.call-start = ((), (), s32[]{:S(2)}) async-start(), calls=%async_computation.3 | async-start | bytes 163840 | tf_op jit(solution)/shard_map/reduce_scatter | solution.py:44
Sparse Core Ops, SparseCore 0:
  12.9 37.0 all-reduce.1
  72.4 19.6 reduce-scatter.1
where the time goes:
time: 115 us; the launch traced here: 114 us
  waiting for transfers between devices  36.5 us (32%)
  blocking collectives  24.2 us (21%)
  local copies, waits for them, and re-layouts  16.8 us (15%)
  between operations  14.1 us (12%)
  matrix products  12.7 us (11%)
  other arithmetic  5.55 us (5%)
  starting transfers between devices  4.52 us (4%)
    psum x1, waiting for transfers between devices, on_device(): query_feat = lax.psum(picked.astype(jnp.bfloat16), 'frame')  36.5 us
    all_gather x1, blocking collectives, on_device(): everyone = lax.all_gather(query_feat, 'track', axis=0, tiled=True)  24.2 us
    div x1, matrix products, on_device(): weights = exp_scores / jnp.sum(exp_scores, axis=2, keepdims=True)  7.01 us
    all_to_all x1, local copies, waits for them, and re-layouts, on_device(): lax.all_to_all(cost_grad, 'track', split_axis=2, concat_axis=1, tiled=True)  4.73 us
    all_to_all x1, starting transfers between devices, on_device(): lax.all_to_all(cost_grad, 'track', split_axis=2, concat_axis=1, tiled=True)  4.44 us
    unnamed x5, local copies, waits for them, and re-layouts  4.12 us
    convert_element_type x1, local copies, waits for them, and re-layouts, on_device(): cost_grad = (weights * (grad_x[:, :, None] * coord_x + grad_y[:, :, None]...  3.77 us
    dot_general x1, matrix products, on_device(): jnp.einsum('tqp,tpc->qc', cost_grad, frames, preferred_element_type=jnp.f...  3.56 us
  transfers between devices with their start and end apart: 3, of which 1 were waited for; matrix products, arithmetic and copies ran while one was open for 13% of the time, Pallas kernels for 0%

commit v1 on v0

--- a/solution.py
+++ b/solution.py
@@ -18,7 +18,7 @@
     row_index = jnp.clip(local_index, 0, held_frames - 1) * pixels + query_pixel
     picked = frames.reshape(held_frames * pixels, channels)[row_index]
     picked = jnp.where(inside[:, None], picked.astype(jnp.float32), 0.0)
-    query_feat = lax.psum(picked.astype(jnp.bfloat16), "frame")
+    query_feat = jnp.sum(lax.all_gather(picked.astype(jnp.bfloat16), "frame"), axis=0)
     score_scale = C ** (-0.5)
     pixel_ids = jnp.arange(pixels)
     coord_x = (pixel_ids % FEAT_W * (2.0 / (FEAT_W - 1)) - 1.0).astype(jnp.float32)

time: 115 us -> 93.4 us (0.81)
  waiting for transfers between devices: 36.5 us -> 0.02 us
  blocking collectives: 24.2 us -> 39.8 us
    psum x1 -> x0, waiting for transfers between devices: 36.5 us -> none  [on_device(): query_feat = lax.psum(picked.astype(jnp.bfloat16), 'frame')]
    all_gather x0 -> x1, blocking collectives: none -> 15.7 us  [on_device(): lax.all_gather(picked.astype(jnp.bfloat16), 'frame')]
    unnamed x5 -> x3, local copies, waits for them, and re-layouts: 4.12 us -> 4.12 us
  transfers between devices with their start and end apart: 3 -> 2, of which waited for: 1 -> 0; matrix products, arithmetic and copies ran while one was open for 13% -> 16% of each run, Pallas kernels for 0% -> 0%
where the time goes in v1:
time: 93.4 us; the launch traced here: 92.9 us
  blocking collectives  39.8 us (43%)
  local copies, waits for them, and re-layouts  16.9 us (18%)
  between operations  14.1 us (15%)
  matrix products  12.6 us (13%)
  other arithmetic  4.96 us (5%)
  starting transfers between devices  4.48 us (5%)
    all_gather x1, blocking collectives, on_device(): everyone = lax.all_gather(query_feat, 'track', axis=0, tiled=True)  24.1 us
    all_gather x1, blocking collectives, on_device(): lax.all_gather(picked.astype(jnp.bfloat16), 'frame')  15.7 us
    div x1, matrix products, on_device(): weights = exp_scores / jnp.sum(exp_scores, axis=2, keepdims=True)  6.95 us
    all_to_all x1, local copies, waits for them, and re-layouts, on_device(): lax.all_to_all(cost_grad, 'track', split_axis=2, concat_axis=1, tiled=True)  4.73 us
    all_to_all x1, starting transfers between devices, on_device(): lax.all_to_all(cost_grad, 'track', split_axis=2, concat_axis=1, tiled=True)  4.44 us
    unnamed x3, local copies, waits for them, and re-layouts  4.12 us
    convert_element_type x1, local copies, waits for them, and re-layouts, on_device(): cost_grad = (weights * (grad_x[:, :, None] * coord_x + grad_y[:, :, None]...  3.77 us
    dot_general x1, matrix products, on_device(): jnp.einsum('tqp,tpc->qc', cost_grad, frames, preferred_element_type=jnp.f...  3.56 us
  transfers between devices with their start and end apart: 2, of which 0 were waited for; matrix products, arithmetic and copies ran while one was open for 16% of the time, Pallas kernels for 0%

profile of v1, /device:TPU:0, one launch (start us, length us, event | category | flops | bytes accessed | tf_op | source)
XLA Modules:
  0.0 92.9 jit_solution(8576543731587749341)
XLA Ops:
  7.2 0.7 compare_and_fusion
  7.9 0.7 compare_select_fusion
  8.5 3.5 %gather_fusion = bf16[128,256]{1,0:T(8,128)(2,1)S(1)} fusion(bf16[8192,256]{1,0:T(8,128)(2,1)} %bitcast.41, s32[1024]{0:T(1024)S(1)} %pad_clamp_fusion), kind=kCustom, calls=%fused_computation | custom fusion | bytes 131584 | tf_op jit(solution)/shard_map/gather | solution.py:19
  12.0 0.1 fusion.7
  12.1 15.7 %all_gather.7 = bf16[4,128,256]{2,1,0:T(8,128)(2,1)S(1)} all-gather(bf16[1,128,256]{2,1,0:T(8,128)(2,1)S(1)} %fusion.7), channel_id=1, replica_groups=mesh['groups'=2,'track'=4,'frame'=4] {'frame'}, dimensions={0}, use_global_device_ids=true | all-gather | bytes 327680 | tf_op jit(solution)/shard_map/all_gather | solution.py:21
  27.8 0.7 slice_bitcast_fusion.1
  28.5 0.0 copy-start
  28.5 7.0 %multiply_reduce_fusion.1 = (f32[2,128]{1,0:T(2,128)S(1)}, f32[2,128]{1,0:T(2,128)S(1)}, f32[2,128,4096]{2,1,0:T(8,128)}) fusion(f32[4096]{0:T(1024)S(1)} %get-tuple-element.11, f32[4096]{0:T(1024)S(1)} %get-tuple-element.12, bf16[2,4096,256]{2,1,0:T(8,128)(2,1)} %param.4, bf16[128,256]{1,0:T(8,128)(2,1)S(1)} %reduce_sum.39), kind=kOutput, calls=%fused_computation.10 | convolution fusion | flops 544219136 | bytes 8488960 | tf_op jit(solution)/shard_map/div | solution.py:32
  35.5 0.0 copy-done
  35.5 3.5 %multiply_convert_fusion = bf16[2,128,4096]{2,1,0:T(8,128)(2,1)S(1)} fusion(f32[2,128,4096]{2,1,0:T(8,128)} %get-tuple-element.10, f32[2,128]{1,0:T(2,128)S(1)} %multiply_add_fusion, f32[4096]{0:T(1024)S(1)} %get-tuple-element.12, f32[2,128]{1,0:T(2,128)S(1)} %get-tuple-element.9, f32[4096]{0:T(1024)S(1)} %get-tuple-element.11, f32[2,128]{1,0:T(2,128)S(1)} %get-tuple-element.8), kind=kLoop, calls=%fused_computation.8 | loop fusion | flops 7340032 | bytes 6327296 | tf_op jit(solution)/shard_map/convert_element_type | solution.py:42
  39.0 3.8 %copy.10 = bf16[2,128,4096]{1,0,2:T(2,128)(2,1)} copy(bf16[2,128,4096]{2,1,0:T(8,128)(2,1)S(1)} %multiply_convert_fusion) | data formatting | bytes 4194304 | tf_op jit(solution)/shard_map/convert_element_type | solution.py:42
  42.7 4.4 %all-to-all-start = ((bf16[2,128,4096]{1,0,2:T(2,128)(2,1)}), bf16[2,128,4096]{1,0,2:T(2,128)(2,1)}, u32[]{:S(2)}, u32[]{:S(2)}) async-start(bf16[2,128,4096]{1,0,2:T(2,128)(2,1)} %copy.10), calls=%async_computation | async-start | bytes 4194304 | tf_op jit(solution)/shard_map/all_to_all | solution.py:48
  47.2 0.0 reduce-scatter.2.cloned.1.call-start
  47.2 3.6 %convolution_bitcast_fusion.1 = f32[128,256]{1,0:T(8,128)} fusion(bf16[2,128,4096]{2,1,0:T(8,128)(2,1)S(1)} %multiply_convert_fusion, bf16[2,4096,256]{2,1,0:T(8,128)(2,1)} %param.4), kind=kOutput, calls=%fused_computation.12 | convolution fusion | flops 536870912 | bytes 6422528 | tf_op jit(solution)/shard_map/tqp,tpc->qc/dot_general | solution.py:43
  50.8 0.0 reduce-scatter.2.cloned.1.call-update
  50.8 0.1 copy.9
  50.9 24.1 %all_gather.8 = bf16[512,256]{0,1:T(8,128)(2,1)S(1)} all-gather(bf16[128,256]{0,1:T(8,128)(2,1)S(1)} %copy.9), channel_id=1, replica_groups=mesh['groups'=2,'track'=4,'frame'=4] {'track'}, dimensions={0}, use_global_device_ids=true | all-gather | bytes 327680 | tf_op jit(solution)/shard_map/all_gather | solution.py:45
  75.1 0.0 all-to-all-done
  75.1 4.7 %copy.11 = bf16[2,128,4,1024]{3,1,2,0:T(8,128)(2,1)S(1)} copy(bf16[2,128,4,1024]{1,0,3,2:T(2,128)(2,1)} %bitcast.7) | data formatting | bytes 4194304 | tf_op jit(solution)/shard_map/all_to_all | solution.py:48
  79.8 2.1 %convolution_bitcast_fusion = f32[1024,2,256]{0,2,1:T(8,128)} fusion(bf16[2,512,1024]{2,1,0:T(8,128)(2,1)S(1)} %bitcast.40, bf16[512,256]{0,1:T(8,128)(2,1)S(1)} %all_gather.8), kind=kOutput, calls=%fused_computation.11 | convolution fusion | flops 536870912 | bytes 4456448 | tf_op jit(solution)/shard_map/tqp,qc->ptc/dot_general | solution.py:46
  81.9 4.1 %copy.12 = f32[1024,2,256]{2,1,0:T(2,128)} copy(f32[1024,2,256]{0,2,1:T(8,128)} %convolution_bitcast_fusion) | data formatting | bytes 4194304
  86.0 0.0 reduce-scatter.2.cloned.1.call-done
  (4 shorter events, 0.1 us)
Async XLA Ops:
  28.5 7.0 %copy-start = (f32[2,2,128]{2,1,0:T(2,128)S(1)}, f32[2,2,128]{2,1,0:T(2,128)}, u32[]{:S(2)}) copy-start(f32[2,2,128]{2,1,0:T(2,128)} %param.7) | copy-start | bytes 6148
  42.7 32.4 %all-to-all-start = ((bf16[2,128,4096]{1,0,2:T(2,128)(2,1)}), bf16[2,128,4096]{1,0,2:T(2,128)(2,1)}, u32[]{:S(2)}, u32[]{:S(2)}) async-start(bf16[2,128,4096]{1,0,2:T(2,128)(2,1)} %copy.10), calls=%async_computation | async-start | bytes 4194304 | tf_op jit(solution)/shard_map/all_to_all | solution.py:48
  47.2 38.8 %reduce-scatter.2.cloned.1.call-start = ((), (), s32[]{:S(2)}) async-start(), calls=%async_computation.2 | async-start | bytes 163840 | tf_op jit(solution)/shard_map/reduce_scatter | solution.py:44
Sparse Core Ops, SparseCore 0:
  50.9 21.4 reduce-scatter.1
